TPU v7x, 32 devices: a whole 2x2x4 slice. The times are simulated.
32 devices in a mesh: dp: 4 (over y, x), feat: 8 (over z, core).
Axes of the slice: x: 2, y: 2, z: 4, core: 2. Of those that a mesh axis runs over, the one named last changes fastest.
Arguments:
- features: bfloat16 [8192, 1024], P('dp', 'feat'), may hold values from -6 to 6
- owners: int32 [8, 64, 1], P('feat', 'dp'), may hold values from 0 to 3; in each aligned block of 16 rows (0 to 15, 16 to 31, ..., all dimensions but the last counted through in order) at most 8 rows name the same one
- weights: bfloat16 [8, 4096], P(None, ('dp', 'feat')), may hold values from -0.1875 to 0.1875
- labels: int32 [8192], P('dp'), may hold values from 0 to 7
Outputs:
- hessian: float32 [32, 1024, 1024], P(('dp', 'feat'))
- gradient: float32 [8, 4096], P(None, ('dp', 'feat'))
Inputs may be any that keep to these rules, and one draw needn't show every extreme that they name: `owners`: among the 16 row blocks of one index of dp, in one tile column, at most 8 name the same owner, a bound that some block reaches.
All inputs are finite; a program needn't handle non-finite values.
Results may differ from a plain program's by a relative error of at most 0.0023.
Values may be sent and summed in bfloat16 or wider, within the bound.
A program may use at most 64 MiB of HBM per device.

v0:
```python
import math

import jax
import jax.numpy as jnp
from jax import lax
from jax.sharding import PartitionSpec as P


def normalize(logits):
    expo = jnp.exp(logits)
    return expo / jnp.sum(expo, axis=-1, keepdims=True)


def spread_diagonal(diag_part, classes, width):
    blocks = diag_part.reshape(classes, width, width)
    unit = jnp.eye(classes, dtype=jnp.float32)
    return (unit[:, None, :, None] * blocks[:, :, None, :]).reshape(
        classes * width, classes * width
    )


def arrange(target, groups, capacity):
    count = target.shape[0]
    order = jnp.arange(count, dtype=jnp.int32)
    earlier = (order[None, :] < order[:, None]) & (target[None, :] == target[:, None])
    ranking = jnp.sum(earlier.astype(jnp.int32), axis=1)
    slot_index = jnp.arange(groups * capacity, dtype=jnp.int32)
    slot_group = slot_index // capacity
    slot_rank = slot_index % capacity
    hits = (target[None, :] == slot_group[:, None]) & (ranking[None, :] == slot_rank[:, None])
    source = jnp.sum(jnp.where(hits, order[None, :], 0), axis=1)
    filled = jnp.any(hits, axis=1)
    return (source, filled)


def select_blocks(block_data, source, filled):
    picked = jnp.take(block_data, source, axis=0)
    return jnp.where(filled[:, None, None], picked, jnp.zeros_like(picked))


def accumulate(totals, feature_rows, prob_rows, classes):
    count, width = feature_rows.shape
    group = math.gcd(count, 512)

    def turn(step, state):
        hess_acc, grad_acc = state
        begin = step * group
        x_part = lax.dynamic_slice_in_dim(feature_rows, begin, group, 0)
        p_part = lax.dynamic_slice_in_dim(prob_rows, begin, group, 0)
        probs = p_part[:, :classes].astype(jnp.float32)
        resid = p_part[:, classes:]
        kron_rows = (
            (probs[:, :, None] * x_part.astype(jnp.float32)[:, None, :])
            .reshape(group, classes * width)
            .astype(jnp.bfloat16)
        )
        joint = jnp.concatenate([kron_rows, x_part], axis=1)
        product = lax.dot_general(
            kron_rows, joint, (((0,), (0,)), ((), ())), preferred_element_type=jnp.float32
        )
        square = product[:, : classes * width]
        diag_part = product[:, classes * width :]
        grad_term = lax.dot_general(
            resid, x_part, (((0,), (0,)), ((), ())), preferred_element_type=jnp.float32
        )
        return (
            hess_acc + spread_diagonal(diag_part, classes, width) - square,
            grad_acc + grad_term,
        )

    return lax.fori_loop(0, count // group, turn, totals)


def per_device(features, owners, weights, labels):
    rows, width = features.shape
    classes = weights.shape[0]
    blocks = owners.shape[1]
    block_rows = rows // blocks
    dp_count = lax.axis_size("dp")
    capacity = max(2, 2 * ((blocks + dp_count - 1) // dp_count))
    target = owners.reshape(blocks)
    gathered = lax.all_gather(weights, "dp", axis=1, tiled=True)
    table = gathered.reshape(classes, dp_count, width)
    every_owner = jnp.einsum("rt,cut->ruc", features, table, preferred_element_type=jnp.float32)
    row_owner = jnp.repeat(target, block_rows)
    owner_mask = (row_owner[:, None] == jnp.arange(dp_count, dtype=jnp.int32)[None, :]).astype(
        jnp.float32
    )
    partial_logits = jnp.sum(every_owner * owner_mask[:, :, None], axis=1)
    logits = lax.psum(partial_logits, "feat")
    probs = normalize(logits)
    onehot = (labels[:, None] == jnp.arange(classes, dtype=jnp.int32)[None, :]).astype(jnp.float32)
    probs_half = probs.astype(jnp.bfloat16)
    resid = (probs - onehot).astype(jnp.bfloat16)
    paired = jnp.concatenate([probs_half, resid], axis=1)
    feature_blocks = features.reshape(blocks, block_rows, width)
    paired_blocks = paired.reshape(blocks, block_rows, 2 * classes)
    start = (
        jnp.zeros((classes * width, classes * width), jnp.float32),
        jnp.zeros((classes, width), jnp.float32),
    )
    source, filled = arrange(target, dp_count, capacity)
    sent_features = select_blocks(feature_blocks, source, filled)
    sent_paired = select_blocks(paired_blocks, source, filled)
    got_features, got_paired = (
        lax.all_to_all(sent_features, "dp", split_axis=0, concat_axis=0, tiled=True),
        lax.all_to_all(sent_paired, "dp", split_axis=0, concat_axis=0, tiled=True),
    )
    hess_acc, grad_acc = accumulate(
        start, got_features.reshape(-1, width), got_paired.reshape(-1, 2 * classes), classes
    )
    hessian = (hess_acc / block_rows)[None]
    gradient = grad_acc / block_rows
    return (hessian, gradient)


def solution(mesh):
    in_specs = (P("dp", "feat"), P("feat", "dp", None), P(None, ("dp", "feat")), P("dp"))
    out_specs = (P(("dp", "feat"), None, None), P(None, ("dp", "feat")))
    return jax.shard_map(
        per_device, mesh=mesh, in_specs=in_specs, out_specs=out_specs, check_vma=False
    )
```

profile of v0, /device:TPU:0, one launch (start us, length us, event | category | flops | bytes accessed | tf_op | source)
XLA Modules:
  0.0 189.6 jit_solution(15932147110795025760)
XLA Ops:
  8.0 9.6 %all_gather.3 = bf16[8,512]{1,0:T(8,128)(2,1)S(1)} all-gather(bf16[8,128]{1,0:T(8,128)(2,1)} %param.8), channel_id=1, replica_groups=mesh['dp'=4,'feat'=8] {'dp'}, dimensions={1}, use_global_device_ids=true | all-gather | bytes 10240 | tf_op jit(solution)/shard_map/all_gather | solution.py:82
  21.8 50.8 %all-reduce.2.cloned.1.call-done = f32[2048,8]{0,1:T(8,128)} async-done(((f32[2048,8]{0,1:T(8,128)}), f32[2048,8]{0,1:T(8,128)}) %all-reduce.2.cloned.1.call-update) | async-done | bytes 65552 | tf_op jit(solution)/shard_map/psum | solution.py:90
  75.8 3.6 %all-to-all-start = ((bf16[32,128,16]{1,2,0:T(8,128)(2,1)}), bf16[32,128,16]{1,2,0:T(8,128)(2,1)S(1)}, u32[]{:S(2)}, u32[]{:S(2)}) async-start(bf16[32,128,16]{1,2,0:T(8,128)(2,1)} %select_select_fusion.1), calls=%async_computation | async-start | bytes 262144 | tf_op jit(solution)/shard_map/all_to_all | solution.py:107
  80.6 3.8 %all-to-all-done = bf16[32,128,16]{1,2,0:T(8,128)(2,1)S(1)} async-done(((bf16[32,128,16]{1,2,0:T(8,128)(2,1)}), bf16[32,128,16]{1,2,0:T(8,128)(2,1)S(1)}, u32[]{:S(2)}, u32[]{:S(2)}) %all-to-all-start) | async-done | bytes 131104 | tf_op jit(solution)/shard_map/all_to_all | solution.py:107
  84.4 3.5 %all-to-all-start.1 = ((bf16[32,128,128]{2,1,0:T(8,128)(2,1)}), bf16[32,128,128]{2,1,0:T(8,128)(2,1)S(1)}, u32[]{:S(2)}, u32[]{:S(2)}) async-start(bf16[32,128,128]{2,1,0:T(8,128)(2,1)} %select_select_fusion), calls=%async_computation.1 | async-start | bytes 2097152 | tf_op jit(solution)/shard_map/all_to_all | solution.py:106
  88.0 10.9 %all-to-all-done.1 = bf16[32,128,128]{2,1,0:T(8,128)(2,1)S(1)} async-done(((bf16[32,128,128]{2,1,0:T(8,128)(2,1)}), bf16[32,128,128]{2,1,0:T(8,128)(2,1)S(1)}, u32[]{:S(2)}, u32[]{:S(2)}) %all-to-all-start.1) | async-done | bytes 1048608 | tf_op jit(solution)/shard_map/all_to_all | solution.py:106
  98.9 78.2 %while.16 = (s32[]{:T(128)}, f32[1024,1024]{1,0:T(8,128)}, f32[8,128]{1,0:T(8,128)S(1)}, bf16[4096,16]{0,1:T(8,128)(2,1)S(1)}, bf16[4096,128]{1,0:T(8,128)(2,1)S...) while((s32[]{:T(128)}, f32[1024,1024]{1,0:T(8,128)}, f32[8,128]{1,0:T(8,128)S(1)}, ...), condition=%wide.region_7.8_spmd.clone, body=%wide.region_6.7_spmd.clone.sunk | while | flops 1216682112 | bytes 66151160 | solution.py:71
  103.9 2.7 %fusion.36 = f32[1024,1024]{1,0:T(8,128)S(1)} fusion(f32[128,8,8,128]{3,2,1,0:T(8,128)S(1)} %bitcast.61, f32[1024,1152]{1,0:T(8,128)S(1)} %fusion.34, f32[1024,1024]{1,0:T(8,128)S(1)} %copy-done.1, pred[]{:T(512)S(6)} %compare.8), kind=kLoop, calls=%fused_computation.3.clone.1 | loop fusion | flops 3145728 | bytes 16777216 | tf_op jit(solution)/shard_map/while/body/eval_jaxpr/sub | solution.py:67
  106.6 2.0 %copy-done.2 = f32[1024,1024]{1,0:T(8,128)} copy-done((f32[1024,1024]{1,0:T(8,128)}, f32[1024,1024]{1,0:T(8,128)S(1)}, u32[]{:S(2)}) %copy-start.2) | copy-done | bytes 4194328 | tf_op jit(solution)/shard_map/while
  113.7 2.7 %fusion.36 = f32[1024,1024]{1,0:T(8,128)S(1)} fusion(f32[128,8,8,128]{3,2,1,0:T(8,128)S(1)} %bitcast.61, f32[1024,1152]{1,0:T(8,128)S(1)} %fusion.34, f32[1024,1024]{1,0:T(8,128)S(1)} %copy-done.1, pred[]{:T(512)S(6)} %compare.8), kind=kLoop, calls=%fused_computation.3.clone.1 | loop fusion | flops 3145728 | bytes 16777216 | tf_op jit(solution)/shard_map/while/body/eval_jaxpr/sub | solution.py:67
  116.4 2.0 %copy-done.2 = f32[1024,1024]{1,0:T(8,128)} copy-done((f32[1024,1024]{1,0:T(8,128)}, f32[1024,1024]{1,0:T(8,128)S(1)}, u32[]{:S(2)}) %copy-start.2) | copy-done | bytes 4194328 | tf_op jit(solution)/shard_map/while
  123.5 2.7 %fusion.36 = f32[1024,1024]{1,0:T(8,128)S(1)} fusion(f32[128,8,8,128]{3,2,1,0:T(8,128)S(1)} %bitcast.61, f32[1024,1152]{1,0:T(8,128)S(1)} %fusion.34, f32[1024,1024]{1,0:T(8,128)S(1)} %copy-done.1, pred[]{:T(512)S(6)} %compare.8), kind=kLoop, calls=%fused_computation.3.clone.1 | loop fusion | flops 3145728 | bytes 16777216 | tf_op jit(solution)/shard_map/while/body/eval_jaxpr/sub | solution.py:67
  126.2 2.0 %copy-done.2 = f32[1024,1024]{1,0:T(8,128)} copy-done((f32[1024,1024]{1,0:T(8,128)}, f32[1024,1024]{1,0:T(8,128)S(1)}, u32[]{:S(2)}) %copy-start.2) | copy-done | bytes 4194328 | tf_op jit(solution)/shard_map/while
  133.3 2.7 %fusion.36 = f32[1024,1024]{1,0:T(8,128)S(1)} fusion(f32[128,8,8,128]{3,2,1,0:T(8,128)S(1)} %bitcast.61, f32[1024,1152]{1,0:T(8,128)S(1)} %fusion.34, f32[1024,1024]{1,0:T(8,128)S(1)} %copy-done.1, pred[]{:T(512)S(6)} %compare.8), kind=kLoop, calls=%fused_computation.3.clone.1 | loop fusion | flops 3145728 | bytes 16777216 | tf_op jit(solution)/shard_map/while/body/eval_jaxpr/sub | solution.py:67
  136.0 2.0 %copy-done.2 = f32[1024,1024]{1,0:T(8,128)} copy-done((f32[1024,1024]{1,0:T(8,128)}, f32[1024,1024]{1,0:T(8,128)S(1)}, u32[]{:S(2)}) %copy-start.2) | copy-done | bytes 4194328 | tf_op jit(solution)/shard_map/while
  143.1 2.7 %fusion.36 = f32[1024,1024]{1,0:T(8,128)S(1)} fusion(f32[128,8,8,128]{3,2,1,0:T(8,128)S(1)} %bitcast.61, f32[1024,1152]{1,0:T(8,128)S(1)} %fusion.34, f32[1024,1024]{1,0:T(8,128)S(1)} %copy-done.1, pred[]{:T(512)S(6)} %compare.8), kind=kLoop, calls=%fused_computation.3.clone.1 | loop fusion | flops 3145728 | bytes 16777216 | tf_op jit(solution)/shard_map/while/body/eval_jaxpr/sub | solution.py:67
  145.8 2.0 %copy-done.2 = f32[1024,1024]{1,0:T(8,128)} copy-done((f32[1024,1024]{1,0:T(8,128)}, f32[1024,1024]{1,0:T(8,128)S(1)}, u32[]{:S(2)}) %copy-start.2) | copy-done | bytes 4194328 | tf_op jit(solution)/shard_map/while
  152.8 2.7 %fusion.36 = f32[1024,1024]{1,0:T(8,128)S(1)} fusion(f32[128,8,8,128]{3,2,1,0:T(8,128)S(1)} %bitcast.61, f32[1024,1152]{1,0:T(8,128)S(1)} %fusion.34, f32[1024,1024]{1,0:T(8,128)S(1)} %copy-done.1, pred[]{:T(512)S(6)} %compare.8), kind=kLoop, calls=%fused_computation.3.clone.1 | loop fusion | flops 3145728 | bytes 16777216 | tf_op jit(solution)/shard_map/while/body/eval_jaxpr/sub | solution.py:67
  155.5 2.0 %copy-done.2 = f32[1024,1024]{1,0:T(8,128)} copy-done((f32[1024,1024]{1,0:T(8,128)}, f32[1024,1024]{1,0:T(8,128)S(1)}, u32[]{:S(2)}) %copy-start.2) | copy-done | bytes 4194328 | tf_op jit(solution)/shard_map/while
  162.6 2.7 %fusion.36 = f32[1024,1024]{1,0:T(8,128)S(1)} fusion(f32[128,8,8,128]{3,2,1,0:T(8,128)S(1)} %bitcast.61, f32[1024,1152]{1,0:T(8,128)S(1)} %fusion.34, f32[1024,1024]{1,0:T(8,128)S(1)} %copy-done.1, pred[]{:T(512)S(6)} %compare.8), kind=kLoop, calls=%fused_computation.3.clone.1 | loop fusion | flops 3145728 | bytes 16777216 | tf_op jit(solution)/shard_map/while/body/eval_jaxpr/sub | solution.py:67
  165.3 2.0 %copy-done.2 = f32[1024,1024]{1,0:T(8,128)} copy-done((f32[1024,1024]{1,0:T(8,128)}, f32[1024,1024]{1,0:T(8,128)S(1)}, u32[]{:S(2)}) %copy-start.2) | copy-done | bytes 4194328 | tf_op jit(solution)/shard_map/while
  172.4 2.7 %fusion.36 = f32[1024,1024]{1,0:T(8,128)S(1)} fusion(f32[128,8,8,128]{3,2,1,0:T(8,128)S(1)} %bitcast.61, f32[1024,1152]{1,0:T(8,128)S(1)} %fusion.34, f32[1024,1024]{1,0:T(8,128)S(1)} %copy-done.1, pred[]{:T(512)S(6)} %compare.8), kind=kLoop, calls=%fused_computation.3.clone.1 | loop fusion | flops 3145728 | bytes 16777216 | tf_op jit(solution)/shard_map/while/body/eval_jaxpr/sub | solution.py:67
  175.1 2.0 %copy-done.2 = f32[1024,1024]{1,0:T(8,128)} copy-done((f32[1024,1024]{1,0:T(8,128)}, f32[1024,1024]{1,0:T(8,128)S(1)}, u32[]{:S(2)}) %copy-start.2) | copy-done | bytes 4194328 | tf_op jit(solution)/shard_map/while
  177.7 5.0 %multiply_bitcast_fusion = f32[1,1024,1024]{2,1,0:T(8,128)} fusion(f32[1024,1024]{1,0:T(8,128)} %get-tuple-element.97), kind=kLoop, calls=%fused_computation.18 | loop fusion | flops 1048576 | bytes 8388608 | tf_op jit(solution)/shard_map/broadcast_in_dim | solution.py:112
  (129 shorter events, 49.9 us)
Async XLA Ops:
  7.2 10.5 %copy-start = (bf16[2048,128]{1,0:T(8,128)(2,1)S(1)}, bf16[2048,128]{1,0:T(8,128)(2,1)}, u32[]{:S(2)}) copy-start(bf16[2048,128]{1,0:T(8,128)(2,1)} %param.6) | copy-start | bytes 1572868
  7.2 65.4 %all-reduce.2.cloned.1.call-start = ((), (), s32[]{:S(2)}) async-start(), calls=%async_computation.2 | async-start | bytes 131072 | tf_op jit(solution)/shard_map/psum | solution.py:90
  75.8 8.7 %all-to-all-start = ((bf16[32,128,16]{1,2,0:T(8,128)(2,1)}), bf16[32,128,16]{1,2,0:T(8,128)(2,1)S(1)}, u32[]{:S(2)}, u32[]{:S(2)}) async-start(bf16[32,128,16]{1,2,0:T(8,128)(2,1)} %select_select_fusion.1), calls=%async_computation | async-start | bytes 262144 | tf_op jit(solution)/shard_map/all_to_all | solution.py:107
  84.4 14.4 %all-to-all-start.1 = ((bf16[32,128,128]{2,1,0:T(8,128)(2,1)}), bf16[32,128,128]{2,1,0:T(8,128)(2,1)S(1)}, u32[]{:S(2)}, u32[]{:S(2)}) async-start(bf16[32,128,128]{2,1,0:T(8,128)(2,1)} %select_select_fusion), calls=%async_computation.1 | async-start | bytes 2097152 | tf_op jit(solution)/shard_map/all_to_all | solution.py:106
  101.7 2.2 %copy-start.1 = (f32[1024,1024]{1,0:T(8,128)S(1)}, f32[1024,1024]{1,0:T(8,128)}, u32[]{:S(2)}) copy-start(f32[1024,1024]{1,0:T(8,128)} %get-tuple-element.179) | copy-start | bytes 12582916 | tf_op jit(solution)/shard_map/while
  106.6 2.0 %copy-start.2 = (f32[1024,1024]{1,0:T(8,128)}, f32[1024,1024]{1,0:T(8,128)S(1)}, u32[]{:S(2)}) copy-start(f32[1024,1024]{1,0:T(8,128)S(1)} %fusion.36) | copy-start | bytes 12582916 | tf_op jit(solution)/shard_map/while
  111.5 2.2 %copy-start.1 = (f32[1024,1024]{1,0:T(8,128)S(1)}, f32[1024,1024]{1,0:T(8,128)}, u32[]{:S(2)}) copy-start(f32[1024,1024]{1,0:T(8,128)} %get-tuple-element.179) | copy-start | bytes 12582916 | tf_op jit(solution)/shard_map/while
  116.4 2.0 %copy-start.2 = (f32[1024,1024]{1,0:T(8,128)}, f32[1024,1024]{1,0:T(8,128)S(1)}, u32[]{:S(2)}) copy-start(f32[1024,1024]{1,0:T(8,128)S(1)} %fusion.36) | copy-start | bytes 12582916 | tf_op jit(solution)/shard_map/while
  121.3 2.2 %copy-start.1 = (f32[1024,1024]{1,0:T(8,128)S(1)}, f32[1024,1024]{1,0:T(8,128)}, u32[]{:S(2)}) copy-start(f32[1024,1024]{1,0:T(8,128)} %get-tuple-element.179) | copy-start | bytes 12582916 | tf_op jit(solution)/shard_map/while
  126.2 2.0 %copy-start.2 = (f32[1024,1024]{1,0:T(8,128)}, f32[1024,1024]{1,0:T(8,128)S(1)}, u32[]{:S(2)}) copy-start(f32[1024,1024]{1,0:T(8,128)S(1)} %fusion.36) | copy-start | bytes 12582916 | tf_op jit(solution)/shard_map/while
  131.1 2.2 %copy-start.1 = (f32[1024,1024]{1,0:T(8,128)S(1)}, f32[1024,1024]{1,0:T(8,128)}, u32[]{:S(2)}) copy-start(f32[1024,1024]{1,0:T(8,128)} %get-tuple-element.179) | copy-start | bytes 12582916 | tf_op jit(solution)/shard_map/while
  136.0 2.0 %copy-start.2 = (f32[1024,1024]{1,0:T(8,128)}, f32[1024,1024]{1,0:T(8,128)S(1)}, u32[]{:S(2)}) copy-start(f32[1024,1024]{1,0:T(8,128)S(1)} %fusion.36) | copy-start | bytes 12582916 | tf_op jit(solution)/shard_map/while
  140.9 2.2 %copy-start.1 = (f32[1024,1024]{1,0:T(8,128)S(1)}, f32[1024,1024]{1,0:T(8,128)}, u32[]{:S(2)}) copy-start(f32[1024,1024]{1,0:T(8,128)} %get-tuple-element.179) | copy-start | bytes 12582916 | tf_op jit(solution)/shard_map/while
  145.8 2.0 %copy-start.2 = (f32[1024,1024]{1,0:T(8,128)}, f32[1024,1024]{1,0:T(8,128)S(1)}, u32[]{:S(2)}) copy-start(f32[1024,1024]{1,0:T(8,128)S(1)} %fusion.36) | copy-start | bytes 12582916 | tf_op jit(solution)/shard_map/while
  150.6 2.2 %copy-start.1 = (f32[1024,1024]{1,0:T(8,128)S(1)}, f32[1024,1024]{1,0:T(8,128)}, u32[]{:S(2)}) copy-start(f32[1024,1024]{1,0:T(8,128)} %get-tuple-element.179) | copy-start | bytes 12582916 | tf_op jit(solution)/shard_map/while
  155.5 2.0 %copy-start.2 = (f32[1024,1024]{1,0:T(8,128)}, f32[1024,1024]{1,0:T(8,128)S(1)}, u32[]{:S(2)}) copy-start(f32[1024,1024]{1,0:T(8,128)S(1)} %fusion.36) | copy-start | bytes 12582916 | tf_op jit(solution)/shard_map/while
  160.4 2.2 %copy-start.1 = (f32[1024,1024]{1,0:T(8,128)S(1)}, f32[1024,1024]{1,0:T(8,128)}, u32[]{:S(2)}) copy-start(f32[1024,1024]{1,0:T(8,128)} %get-tuple-element.179) | copy-start | bytes 12582916 | tf_op jit(solution)/shard_map/while
  165.3 2.0 %copy-start.2 = (f32[1024,1024]{1,0:T(8,128)}, f32[1024,1024]{1,0:T(8,128)S(1)}, u32[]{:S(2)}) copy-start(f32[1024,1024]{1,0:T(8,128)S(1)} %fusion.36) | copy-start | bytes 12582916 | tf_op jit(solution)/shard_map/while
  170.2 2.2 %copy-start.1 = (f32[1024,1024]{1,0:T(8,128)S(1)}, f32[1024,1024]{1,0:T(8,128)}, u32[]{:S(2)}) copy-start(f32[1024,1024]{1,0:T(8,128)} %get-tuple-element.179) | copy-start | bytes 12582916 | tf_op jit(solution)/shard_map/while
  175.1 2.0 %copy-start.2 = (f32[1024,1024]{1,0:T(8,128)}, f32[1024,1024]{1,0:T(8,128)S(1)}, u32[]{:S(2)}) copy-start(f32[1024,1024]{1,0:T(8,128)S(1)} %fusion.36) | copy-start | bytes 12582916 | tf_op jit(solution)/shard_map/while
Sparse Core Ops, SparseCore 0:
  18.7 53.8 all-reduce.1
where the time goes:
time: 190 us
  waiting for transfers between devices  65.6 us (35%)
  other arithmetic  42.1 us (22%)
  local copies, waits for them, and re-layouts  35.8 us (19%)
  matrix products  14.6 us (8%)
  between operations  14.1 us (7%)
  blocking collectives  9.63 us (5%)
  starting transfers between devices  7.2 us (4%)
    psum x1, waiting for transfers between devices, per_device(): logits = lax.psum(partial_logits, 'feat')  50.8 us
    while x40, local copies, waits for them, and re-layouts  32.4 us
    sub x8, other arithmetic, turn(): hess_acc + spread_diagonal(diag_part, classes, width) - square  21.6 us
    dot_general x8, matrix products, turn(): lax.dot_general(kron_rows, joint, (((0,), (0,)), ((), ())), preferred_ele...  12.6 us
    all_to_all x1, waiting for transfers between devices, per_device(): lax.all_to_all(sent_features, 'dp', split_axis=0, concat_axis=0, tiled=True)  10.9 us
    all_gather x1, blocking collectives, per_device(): gathered = lax.all_gather(weights, 'dp', axis=1, tiled=True)  9.63 us
    convert_element_type x8, other arithmetic, turn(): kron_rows = (probs[:, :, None] * x_part.astype(jnp.float32)[:, None, :])....  5.53 us
    broadcast_in_dim x1, other arithmetic, per_device(): hessian = (hess_acc / block_rows)[None]  5.04 us
  transfers between devices with their start and end apart: 3, of which 3 were waited for; matrix products, arithmetic and copies ran while one was open for 2% of the time, Pallas kernels for 0%

commit v1 on v0

v1 whole, which is shorter than its diff:
```python
import functools

import jax
import jax.numpy as jnp
from jax import lax
from jax.experimental import pallas as pl
from jax.experimental.pallas import tpu as pltpu
from jax.sharding import PartitionSpec as P

MESH = pl.DeviceIdType.MESH
NT = (((1,), (1,)), ((), ()))


def exchange_kernel(
    dp, feat, capacity,
    owner_ref, x_ref, w_ref, label_ref,
    xt_ref, pt_ref,
    chain, source, table, sent_x, got_x, part, got_part, joint, sent_p, got_p,
    w_send, w_recv, x_send, x_recv, l_send, l_recv, j_send, j_recv, p_send, p_recv,
):
    blocks, block_rows, width = x_ref.shape
    classes = w_ref.shape[0]
    per_feat = blocks // feat
    row = lax.axis_index("dp")
    col = lax.axis_index("feat")

    def dp_peer(offset):
        return (lax.rem(row + offset, dp), col)

    def feat_peer(offset):
        return (row, lax.rem(col + offset, feat))

    barrier = pltpu.get_barrier_semaphore()
    for offset in range(1, dp):
        pl.semaphore_signal(barrier, inc=1, device_id=dp_peer(offset), device_id_type=MESH)
    for offset in range(1, feat):
        pl.semaphore_signal(barrier, inc=1, device_id=feat_peer(offset), device_id_type=MESH)

    heads = [jnp.int32(blocks)] * dp
    chain[blocks] = jnp.int32(blocks)
    for block in reversed(range(blocks)):
        away = lax.rem(owner_ref[block] - row + dp, dp)
        follower = heads[0]
        for offset in range(1, dp):
            follower = jnp.where(away == offset, heads[offset], follower)
        chain[block] = follower
        heads = [jnp.where(away == offset, block, heads[offset]) for offset in range(dp)]
    for offset in range(dp):
        at = heads[offset]
        for k in range(capacity):
            source[offset * capacity + k] = at
            at = chain[at]

    for offset in range(1, dp):
        for k in range(capacity):
            at = jnp.minimum(source[offset * capacity + k], blocks - 1)
            sent_x[offset, k] = x_ref[at]
    table[0] = w_ref[...]

    pl.semaphore_wait(barrier, dp - 1 + feat - 1)

    w_copies, x_copies = [], []
    for offset in range(1, dp):
        copy = pltpu.make_async_remote_copy(
            src_ref=w_ref, dst_ref=table.at[offset],
            send_sem=w_send.at[offset], recv_sem=w_recv.at[offset],
            device_id=dp_peer(offset), device_id_type=MESH,
        )
        copy.start()
        w_copies.append(copy)
    for offset in range(1, dp):
        copy = pltpu.make_async_remote_copy(
            src_ref=sent_x.at[offset], dst_ref=got_x.at[offset],
            send_sem=x_send.at[offset], recv_sem=x_recv.at[offset],
            device_id=dp_peer(offset), device_id_type=MESH,
        )
        copy.start()
        x_copies.append(copy)

    for k in range(capacity):
        at = jnp.minimum(source[k], blocks - 1)
        xt_ref[:, k * block_rows:(k + 1) * block_rows] = x_ref[at].T

    for copy in w_copies:
        copy.wait()

    for block in range(blocks):
        w_block = table[lax.rem(row - owner_ref[block] + dp, dp)]
        part[block] = lax.dot_general(
            w_block, x_ref[block], NT, preferred_element_type=jnp.float32
        )

    l_copies = []
    for offset in range(1, feat):
        to = lax.rem(col + offset, feat)
        copy = pltpu.make_async_remote_copy(
            src_ref=part.at[pl.ds(to * per_feat, per_feat)], dst_ref=got_part.at[offset],
            send_sem=l_send.at[offset], recv_sem=l_recv.at[offset],
            device_id=feat_peer(offset), device_id_type=MESH,
        )
        copy.start()
        l_copies.append(copy)
    for copy in l_copies:
        copy.wait()

    for i in range(per_feat):
        block = col * per_feat + i
        logits = part[block]
        for offset in range(1, feat):
            logits = logits + got_part[offset, i]
        expo = jnp.exp(logits)
        probs = expo / jnp.sum(expo, axis=0, keepdims=True)
        label = label_ref[pl.ds(block, 1), :]
        onehot = lax.broadcasted_iota(jnp.int32, probs.shape, 0) == label
        resid = probs - onehot.astype(jnp.float32)
        joint[block] = jnp.concatenate([probs, resid], axis=0).astype(jnp.bfloat16)

    j_copies = []
    mine = pl.ds(col * per_feat, per_feat)
    for offset in range(1, feat):
        copy = pltpu.make_async_remote_copy(
            src_ref=joint.at[mine], dst_ref=joint.at[mine],
            send_sem=j_send.at[offset], recv_sem=j_recv.at[offset],
            device_id=feat_peer(offset), device_id_type=MESH,
        )
        copy.start()
        j_copies.append(copy)
    for offset in range(1, feat):
        j_copies[offset - 1].wait_send()
        came = lax.rem(col - offset + feat, feat)
        theirs = pl.ds(came * per_feat, per_feat)
        pltpu.make_async_remote_copy(
            src_ref=joint.at[theirs], dst_ref=joint.at[theirs],
            send_sem=j_send.at[offset], recv_sem=j_recv.at[offset],
            device_id=feat_peer(offset), device_id_type=MESH,
        ).wait_recv()

    def picked(offset, k):
        at = source[offset * capacity + k]
        tile = joint[jnp.minimum(at, blocks - 1)]
        return jnp.where(at < blocks, tile, jnp.zeros_like(tile))

    p_copies = []
    for offset in range(1, dp):
        for k in range(capacity):
            sent_p[offset, k] = picked(offset, k)
        copy = pltpu.make_async_remote_copy(
            src_ref=sent_p.at[offset], dst_ref=got_p.at[offset],
            send_sem=p_send.at[offset], recv_sem=p_recv.at[offset],
            device_id=dp_peer(offset), device_id_type=MESH,
        )
        copy.start()
        p_copies.append(copy)
    for k in range(capacity):
        pt_ref[:, k * block_rows:(k + 1) * block_rows] = picked(0, k)

    for offset in range(1, dp):
        x_copies[offset - 1].wait()
        for k in range(capacity):
            begin = (offset * capacity + k) * block_rows
            xt_ref[:, begin:begin + block_rows] = got_x[offset, k].T
    for offset in range(1, dp):
        p_copies[offset - 1].wait()
        for k in range(capacity):
            begin = (offset * capacity + k) * block_rows
            pt_ref[:, begin:begin + block_rows] = got_p[offset, k]


def hessian_kernel(classes, scale, xt_ref, pt_ref, hess_ref, grad_ref, kron, acc, sems):
    width, rows = xt_ref.shape
    pair = 2 * width
    tiles = classes // 2
    lanes = 512

    def build(c):
        for begin in range(0, rows, lanes):
            p_row = pt_ref[c:c + 1, begin:begin + lanes]
            kron[c * width:(c + 1) * width, begin:begin + lanes] = (
                p_row * xt_ref[:, begin:begin + lanes]
            )

    copies = []

    def write(r0, r1, c0, c1):
        copy = pltpu.make_async_copy(
            acc.at[r0:r1, c0:c1], hess_ref.at[0, r0:r1, c0:c1], sems.at[len(copies)]
        )
        copy.start()
        copies.append(copy)

    grad_ref[...] = scale * lax.dot_general(
        pt_ref[...], xt_ref[...], NT, preferred_element_type=jnp.float32
    )[classes:]
    for n in range(tiles):
        build(2 * n)
        build(2 * n + 1)
        low, high = n * pair, (n + 1) * pair
        right = kron[low:high, :]
        for m in range(n + 1):
            square = lax.dot_general(
                kron[m * pair:(m + 1) * pair, :], right, NT, preferred_element_type=jnp.float32
            )
            value = square * (-scale)
            acc[m * pair:(m + 1) * pair, low:high] = value
            if m < n:
                acc[low:high, m * pair:(m + 1) * pair] = value.T
        diag = lax.dot_general(xt_ref[...], right, NT, preferred_element_type=jnp.float32) * scale
        for half in range(2):
            b0 = low + half * width
            acc[b0:b0 + width, b0:b0 + width] += diag[:, half * width:(half + 1) * width].T
        write(0, high, low, high)
        if n > 0:
            write(low, high, 0, low)
    for copy in copies:
        copy.wait()


def per_device(dp, feat, features, owners, weights, labels):
    rows, width = features.shape
    classes = weights.shape[0]
    blocks = owners.shape[1]
    block_rows = rows // blocks
    capacity = max(2, 2 * ((blocks + dp - 1) // dp))
    total = dp * capacity * block_rows
    per_feat = blocks // feat
    bf16, f32 = jnp.bfloat16, jnp.float32
    vmem = pl.BlockSpec(memory_space=pltpu.VMEM)
    dma = pltpu.SemaphoreType.DMA
    x_t, p_t = pl.pallas_call(
        functools.partial(exchange_kernel, dp, feat, capacity),
        out_shape=(
            jax.ShapeDtypeStruct((width, total), bf16),
            jax.ShapeDtypeStruct((2 * classes, total), bf16),
        ),
        in_specs=[pl.BlockSpec(memory_space=pltpu.SMEM), vmem, vmem, vmem],
        out_specs=(vmem, vmem),
        scratch_shapes=[
            pltpu.SMEM((blocks + 1,), jnp.int32),
            pltpu.SMEM((dp * capacity,), jnp.int32),
            pltpu.VMEM((dp, classes, width), bf16),
            pltpu.VMEM((dp, capacity, block_rows, width), bf16),
            pltpu.VMEM((dp, capacity, block_rows, width), bf16),
            pltpu.VMEM((blocks, classes, block_rows), f32),
            pltpu.VMEM((feat, per_feat, classes, block_rows), f32),
            pltpu.VMEM((blocks, 2 * classes, block_rows), bf16),
            pltpu.VMEM((dp, capacity, 2 * classes, block_rows), bf16),
            pltpu.VMEM((dp, capacity, 2 * classes, block_rows), bf16),
            dma((dp,)), dma((dp,)), dma((dp,)), dma((dp,)),
            dma((feat,)), dma((feat,)), dma((feat,)), dma((feat,)),
            dma((dp,)), dma((dp,)),
        ],
        compiler_params=pltpu.CompilerParams(
            collective_id=0, has_side_effects=True, vmem_limit_bytes=24 << 20
        ),
        name="exchange",
    )(
        owners.reshape(blocks),
        features.reshape(blocks, block_rows, width),
        weights,
        labels.reshape(blocks, block_rows),
    )
    size = classes * width
    return pl.pallas_call(
        functools.partial(hessian_kernel, classes, 1.0 / block_rows),
        out_shape=(
            jax.ShapeDtypeStruct((1, size, size), f32),
            jax.ShapeDtypeStruct((classes, width), f32),
        ),
        in_specs=[vmem, vmem],
        out_specs=(pl.BlockSpec(memory_space=pl.ANY), vmem),
        scratch_shapes=[
            pltpu.VMEM((size, total), bf16),
            pltpu.VMEM((size, size), f32),
            dma((classes,)),
        ],
        compiler_params=pltpu.CompilerParams(vmem_limit_bytes=40 << 20),
        name="hessian",
    )(x_t, p_t)


def solution(mesh):
    in_specs = (P("dp", "feat"), P("feat", "dp", None), P(None, ("dp", "feat")), P("dp"))
    out_specs = (P(("dp", "feat"), None, None), P(None, ("dp", "feat")))
    return jax.shard_map(
        functools.partial(per_device, mesh.shape["dp"], mesh.shape["feat"]),
        mesh=mesh, in_specs=in_specs, out_specs=out_specs, check_vma=False,
    )
```

time: 190 us -> 37.4 us (0.20)
  waiting for transfers between devices: 65.6 us -> 0 us
  other arithmetic: 42.1 us -> 0 us
  Pallas kernels: 0 us -> 33.4 us
  local copies, waits for them, and re-layouts: 35.8 us -> 3.07 us
  matrix products: 14.6 us -> 0 us
  between operations: 14.1 us -> 0.65 us
  blocking collectives: 9.63 us -> 0 us
  starting transfers between devices: 7.2 us -> 0 us
    psum x1 -> x0, waiting for transfers between devices: 50.8 us -> none  [per_device(): logits = lax.psum(partial_logits, 'feat')]
    pallas_call x0 -> x2, Pallas kernels: none -> 33.4 us  [the longest x1 23.3 us: per_device(): pl.pallas_call(functools.partial(exchange_kernel, dp, feat, capacity), ou...]
    while x40 -> x0, local copies, waits for them, and re-layouts: 32.4 us -> none
    sub x8 -> x0, other arithmetic: 21.6 us -> none  [turn(): hess_acc + spread_diagonal(diag_part, classes, width) - square]
    all_to_all x2 -> x0, waiting for transfers between devices: 14.7 us -> none  [the longest x1 10.9 us: per_device(): lax.all_to_all(sent_features, 'dp', split_axis=0, concat_axis=0, tiled=True)]
    dot_general x17 -> x0, matrix products: 14.6 us -> none  [the longest x8 12.6 us: turn(): lax.dot_general(kron_rows, joint, (((0,), (0,)), ((), ())), preferred_ele...]
    all_gather x1 -> x0, blocking collectives: 9.63 us -> none  [per_device(): gathered = lax.all_gather(weights, 'dp', axis=1, tiled=True)]
    all_to_all x2 -> x0, starting transfers between devices: 7.16 us -> none  [the longest x1 3.65 us: per_device(): lax.all_to_all(sent_paired, 'dp', split_axis=0, concat_axis=0, tiled=True)]
  transfers between devices with their start and end apart: 3 -> 0, of which waited for: 3 -> 0; matrix products, arithmetic and copies ran while one was open for 2% -> 0% of each run, Pallas kernels for 0% -> 0%
where the time goes in v1:
time: 37.4 us; the launch traced here: 37.2 us
  Pallas kernels  33.4 us (89%)
  local copies, waits for them, and re-layouts  3.07 us (8%)
  between operations  0.65 us (2%)
    pallas_call x1, Pallas kernels, per_device(): pl.pallas_call(functools.partial(exchange_kernel, dp, feat, capacity), ou...  23.3 us
    pallas_call x1, Pallas kernels, per_device(): pl.pallas_call(functools.partial(hessian_kernel, classes, 1.0 / block_row...  10.2 us
    unnamed x8, local copies, waits for them, and re-layouts  3.07 us

profile of v1, /device:TPU:0, one launch (start us, length us, event | category | flops | bytes accessed | tf_op | source)
XLA Modules:
  0.0 37.2 jit_solution(625601222488105592)
XLA Ops:
  0.6 0.0 copy-start
  0.6 1.0 %copy-done = bf16[2048,128]{1,0:T(8,128)(2,1)S(1)} copy-done((bf16[2048,128]{1,0:T(8,128)(2,1)S(1)}, bf16[2048,128]{1,0:T(8,128)(2,1)}, u32[]{:S(2)}) %copy-start) | copy-done | bytes 524312
  1.7 0.0 copy-start.1
  1.7 0.7 %copy-done.1 = s32[2048]{0:T(1024)S(1)} copy-done((s32[2048]{0:T(1024)S(1)}, s32[2048]{0:T(1024)}, u32[]{:S(2)}) %copy-start.1) | copy-done | bytes 8216
  2.4 0.0 copy-start.2
  2.4 0.7 %copy-done.2 = bf16[8,128]{1,0:T(8,128)(2,1)S(1)} copy-done((bf16[8,128]{1,0:T(8,128)(2,1)S(1)}, bf16[8,128]{1,0:T(8,128)(2,1)}, u32[]{:S(2)}) %copy-start.2) | copy-done | bytes 2072
  3.1 0.0 copy-start.3
  3.1 0.7 %copy-done.3 = s32[1,16,1]{1,2,0:T(1,128)S(1)} copy-done((s32[1,16,1]{1,2,0:T(1,128)S(1)}, s32[1,16,1]{1,2,0:T(1,128)}, u32[]{:S(2)}) %copy-start.3) | copy-done | bytes 88
  3.7 23.3 %exchange.1 = (bf16[128,4096]{1,0:T(8,128)(2,1)S(1)}, bf16[16,4096]{1,0:T(8,128)(2,1)S(1)}) custom-call(s32[16]{0:T(128)S(1)} %bitcast.5, bf16[16,128,128]{2,1,0:T(8,128)(2,1)S(1)} %bitcast.3, bf16[8,128]{1,0:T(8,128)(2,1)S(1)} %copy-done.2, s32[16,128]{1,0:T(8,128)S(1)} %bitcast.4), custom_call_target="tpu_custom_call" | custom-call | tf_op jit(solution)/shard_map/exchange/pallas_call | solution.py:229
  27.0 10.2 %hessian.1 = (f32[1,1024,1024]{2,1,0:T(8,128)}, f32[8,128]{1,0:T(8,128)}) custom-call(bf16[128,4096]{1,0:T(8,128)(2,1)S(1)} %get-tuple-element.4.xt_ref, bf16[16,4096]{1,0:T(8,128)(2,1)S(1)} %get-tuple-element.5.pt_ref), custom_call_target="tpu_custom_call" | custom-call | tf_op jit(solution)/shard_map/hessian/pallas_call | solution.py:263
Async XLA Ops:
  0.6 1.0 %copy-start = (bf16[2048,128]{1,0:T(8,128)(2,1)S(1)}, bf16[2048,128]{1,0:T(8,128)(2,1)}, u32[]{:S(2)}) copy-start(bf16[2048,128]{1,0:T(8,128)(2,1)} %param.4) | copy-start | bytes 1572868
  1.7 0.7 %copy-start.1 = (s32[2048]{0:T(1024)S(1)}, s32[2048]{0:T(1024)}, u32[]{:S(2)}) copy-start(s32[2048]{0:T(1024)} %param.7) | copy-start | bytes 24580
  2.4 0.7 %copy-start.2 = (bf16[8,128]{1,0:T(8,128)(2,1)S(1)}, bf16[8,128]{1,0:T(8,128)(2,1)}, u32[]{:S(2)}) copy-start(bf16[8,128]{1,0:T(8,128)(2,1)} %w_ref.1) | copy-start | bytes 6148
  3.1 0.7 %copy-start.3 = (s32[1,16,1]{1,2,0:T(1,128)S(1)}, s32[1,16,1]{1,2,0:T(1,128)}, u32[]{:S(2)}) copy-start(s32[1,16,1]{1,2,0:T(1,128)} %param.5) | copy-start | bytes 196

commit v2 on v1

--- a/solution.py
+++ b/solution.py
@@ -13,13 +13,13 @@
 
 def exchange_kernel(
     dp, feat, capacity,
-    owner_ref, x_ref, w_ref, label_ref,
+    owner_ref, x_hbm, w_hbm, label_hbm,
     xt_ref, pt_ref,
-    chain, source, table, sent_x, got_x, part, got_part, joint, sent_p, got_p,
+    x_ref, label_ref, in_sems, chain, source, table, sent_x, got_x, part, got_part, joint, sent_p, got_p,
     w_send, w_recv, x_send, x_recv, l_send, l_recv, j_send, j_recv, p_send, p_recv,
 ):
     blocks, block_rows, width = x_ref.shape
-    classes = w_ref.shape[0]
+    classes = w_hbm.shape[0]
     per_feat = blocks // feat
     row = lax.axis_index("dp")
     col = lax.axis_index("feat")
@@ -30,6 +30,12 @@
     def feat_peer(offset):
         return (row, lax.rem(col + offset, feat))
 
+    x_load = pltpu.make_async_copy(x_hbm, x_ref, in_sems.at[0])
+    w_load = pltpu.make_async_copy(w_hbm, table.at[0], in_sems.at[1])
+    label_load = pltpu.make_async_copy(label_hbm, label_ref, in_sems.at[2])
+    x_load.start()
+    w_load.start()
+    label_load.start()
     barrier = pltpu.get_barrier_semaphore()
     for offset in range(1, dp):
         pl.semaphore_signal(barrier, inc=1, device_id=dp_peer(offset), device_id_type=MESH)
@@ -51,18 +57,20 @@
             source[offset * capacity + k] = at
             at = chain[at]
 
+    x_load.wait()
+    w_load.wait()
+    label_load.wait()
     for offset in range(1, dp):
         for k in range(capacity):
             at = jnp.minimum(source[offset * capacity + k], blocks - 1)
             sent_x[offset, k] = x_ref[at]
-    table[0] = w_ref[...]
 
     pl.semaphore_wait(barrier, dp - 1 + feat - 1)
 
     w_copies, x_copies = [], []
     for offset in range(1, dp):
         copy = pltpu.make_async_remote_copy(
-            src_ref=w_ref, dst_ref=table.at[offset],
+            src_ref=table.at[0], dst_ref=table.at[offset],
             send_sem=w_send.at[offset], recv_sem=w_recv.at[offset],
             device_id=dp_peer(offset), device_id_type=MESH,
         )
@@ -225,6 +233,7 @@
     per_feat = blocks // feat
     bf16, f32 = jnp.bfloat16, jnp.float32
     vmem = pl.BlockSpec(memory_space=pltpu.VMEM)
+    hbm = pl.BlockSpec(memory_space=pltpu.HBM)
     dma = pltpu.SemaphoreType.DMA
     x_t, p_t = pl.pallas_call(
         functools.partial(exchange_kernel, dp, feat, capacity),
@@ -232,9 +241,12 @@
             jax.ShapeDtypeStruct((width, total), bf16),
             jax.ShapeDtypeStruct((2 * classes, total), bf16),
         ),
-        in_specs=[pl.BlockSpec(memory_space=pltpu.SMEM), vmem, vmem, vmem],
+        in_specs=[pl.BlockSpec(memory_space=pltpu.SMEM), hbm, hbm, hbm],
         out_specs=(vmem, vmem),
         scratch_shapes=[
+            pltpu.VMEM((blocks, block_rows, width), bf16),
+            pltpu.VMEM((blocks, block_rows), jnp.int32),
+            dma((3,)),
             pltpu.SMEM((blocks + 1,), jnp.int32),
             pltpu.SMEM((dp * capacity,), jnp.int32),
             pltpu.VMEM((dp, classes, width), bf16),

time: 37.4 us -> 37.5 us (level)
  no operation moved by 1% of the time
where the time goes in v2:
time: 37.5 us; the launch traced here: 37.2 us
  Pallas kernels  33.5 us (89%)
  local copies, waits for them, and re-layouts  3.07 us (8%)
  between operations  0.65 us (2%)
    pallas_call x1, Pallas kernels, per_device(): pl.pallas_call(functools.partial(exchange_kernel, dp, feat, capacity), ou...  23.3 us
    pallas_call x1, Pallas kernels, per_device(): pl.pallas_call(functools.partial(hessian_kernel, classes, 1.0 / block_row...  10.2 us
    unnamed x8, local copies, waits for them, and re-layouts  3.07 us

profile of v2, /device:TPU:0, one launch (start us, length us, event | category | flops | bytes accessed | tf_op | source)
XLA Modules:
  0.0 37.2 jit_solution(1811200600104045645)
XLA Ops:
  0.6 0.0 copy-start
  0.6 1.0 %copy-done = bf16[2048,128]{1,0:T(8,128)(2,1)S(1)} copy-done((bf16[2048,128]{1,0:T(8,128)(2,1)S(1)}, bf16[2048,128]{1,0:T(8,128)(2,1)}, u32[]{:S(2)}) %copy-start) | copy-done | bytes 524312
  1.7 0.0 copy-start.1
  1.7 0.7 %copy-done.1 = s32[2048]{0:T(1024)S(1)} copy-done((s32[2048]{0:T(1024)S(1)}, s32[2048]{0:T(1024)}, u32[]{:S(2)}) %copy-start.1) | copy-done | bytes 8216
  2.4 0.0 copy-start.2
  2.4 0.7 %copy-done.2 = bf16[8,128]{1,0:T(8,128)(2,1)S(1)} copy-done((bf16[8,128]{1,0:T(8,128)(2,1)S(1)}, bf16[8,128]{1,0:T(8,128)(2,1)}, u32[]{:S(2)}) %copy-start.2) | copy-done | bytes 2072
  3.1 0.0 copy-start.3
  3.1 0.7 %copy-done.3 = s32[1,16,1]{1,2,0:T(1,128)S(1)} copy-done((s32[1,16,1]{1,2,0:T(1,128)S(1)}, s32[1,16,1]{1,2,0:T(1,128)}, u32[]{:S(2)}) %copy-start.3) | copy-done | bytes 88
  3.7 23.3 %exchange.1 = (bf16[128,4096]{1,0:T(8,128)(2,1)S(1)}, bf16[16,4096]{1,0:T(8,128)(2,1)S(1)}) custom-call(s32[16]{0:T(128)S(1)} %bitcast.5, bf16[16,128,128]{2,1,0:T(8,128)(2,1)S(1)} %bitcast.3, bf16[8,128]{1,0:T(8,128)(2,1)S(1)} %copy-done.2, s32[16,128]{1,0:T(8,128)S(1)} %bitcast.4), custom_call_target="tpu_custom_call" | custom-call | tf_op jit(solution)/shard_map/exchange/pallas_call | solution.py:238
  27.1 10.2 %hessian.1 = (f32[1,1024,1024]{2,1,0:T(8,128)}, f32[8,128]{1,0:T(8,128)}) custom-call(bf16[128,4096]{1,0:T(8,128)(2,1)S(1)} %get-tuple-element.4.xt_ref, bf16[16,4096]{1,0:T(8,128)(2,1)S(1)} %get-tuple-element.5.pt_ref), custom_call_target="tpu_custom_call" | custom-call | tf_op jit(solution)/shard_map/hessian/pallas_call | solution.py:275
Async XLA Ops:
  0.6 1.0 %copy-start = (bf16[2048,128]{1,0:T(8,128)(2,1)S(1)}, bf16[2048,128]{1,0:T(8,128)(2,1)}, u32[]{:S(2)}) copy-start(bf16[2048,128]{1,0:T(8,128)(2,1)} %param.4) | copy-start | bytes 1572868
  1.7 0.7 %copy-start.1 = (s32[2048]{0:T(1024)S(1)}, s32[2048]{0:T(1024)}, u32[]{:S(2)}) copy-start(s32[2048]{0:T(1024)} %param.7) | copy-start | bytes 24580
  2.4 0.7 %copy-start.2 = (bf16[8,128]{1,0:T(8,128)(2,1)S(1)}, bf16[8,128]{1,0:T(8,128)(2,1)}, u32[]{:S(2)}) copy-start(bf16[8,128]{1,0:T(8,128)(2,1)} %w_hbm.1) | copy-start | bytes 6148
  3.1 0.7 %copy-start.3 = (s32[1,16,1]{1,2,0:T(1,128)S(1)}, s32[1,16,1]{1,2,0:T(1,128)}, u32[]{:S(2)}) copy-start(s32[1,16,1]{1,2,0:T(1,128)} %param.5) | copy-start | bytes 196
